TPU v7x, 32 devices: a whole 2x2x4 slice. The times are simulated.
32 devices in a mesh: replica: 8 (over y, x, core), tensor: 4 (over z).
Axes of the slice: x: 2, y: 2, z: 4, core: 2. Of those that a mesh axis runs over, the one named last changes fastest.
Arguments:
- weights: bfloat16 [8, 8192, 2048], P('replica', 'tensor'), may hold values from -6 to 6
- hidden: bfloat16 [8, 512, 8192], P('replica', None, 'tensor'), may hold values from -6 to 6
- out_grad: bfloat16 [8, 512, 2048], P('replica', None, 'tensor'), may hold values from -0.375 to 0.375
- factor_start: bfloat16 [2, 64, 8192], P(None, None, 'tensor'), may hold values from -6 to 6
- matching: int32 [2], replicated, may hold values from 1 to 7, as said below
Outputs:
- new_weights: bfloat16 [8, 8192, 2048], P('replica', 'tensor')
Inputs may be any that keep to these rules, and one draw needn't show every extreme that they name: In step t replica i is matched with replica i XOR matching[t]; in one of the steps matching equals 7.
All inputs are finite; a program needn't handle non-finite values.
Results may differ from a plain program's by a relative error of at most 0.014.
Values may be sent and summed in bfloat16 or wider, within the bound.
No kernel may reach another device: no remote copies, remote signals or barrier semaphores. Data moves between devices by JAX's collectives and lax.ppermute only.
A program may use at most 128 MiB of HBM per device.

v0:
```python
import jax
import jax.numpy as jnp
from jax import lax
from jax.sharding import PartitionSpec as P

STEPS = 2
TOK = 256
learn_rate = 0.1
momentum_decay = 0.9


def from_partner(value, axis, bit):
    mask = 2**bit
    pairs = [(source, source ^ mask) for source in range(lax.axis_size(axis))]
    return lax.ppermute(value, axis, pairs)


def swap_left_side(payload, pairing):
    for bit_number in range(lax.axis_size("replica").bit_length() - 1):
        arrived = from_partner(payload.astype(jnp.bfloat16), "replica", bit_number).astype(
            payload.dtype
        )
        chosen = pairing // 2**bit_number % 2
        payload = jnp.where(chosen == 1, arrived, payload)
    return payload


def swap_right_side(payload, pairing):
    for bit_number in range(lax.axis_size("replica").bit_length() - 1):
        arrived = from_partner(payload.astype(jnp.bfloat16), "replica", bit_number).astype(
            payload.dtype
        )
        chosen = pairing // 2**bit_number % 2
        payload = jnp.where(chosen == 1, arrived, payload)
    return payload


def orthonormal(gram_matrix, difference):
    lower_factor = jnp.linalg.cholesky(gram_matrix)
    return lax.linalg.triangular_solve(lower_factor, difference, left_side=True, lower=True)


def per_device(weights, hidden, out_grad, factor_start, matching):
    current = weights[0]
    hidden_all = hidden[0]
    grads_all = out_grad[0]
    momentum = None
    for step_index in range(STEPS):
        hidden_step = hidden_all[step_index * TOK : (step_index + 1) * TOK]
        grads_step = grads_all[step_index * TOK : (step_index + 1) * TOK]
        gradient = lax.dot_general(
            hidden_step,
            lax.all_gather(grads_step, "tensor", axis=1, tiled=True),
            (((0,), (0,)), ((), ())),
            preferred_element_type=jnp.float32,
        )
        if momentum is None:
            momentum = gradient
        else:
            momentum = momentum_decay * momentum + gradient
        updated = (current.astype(jnp.float32) - learn_rate * momentum).astype(jnp.bfloat16)
        start_factor = factor_start[step_index]
        pairing = matching[step_index]
        local_left = jnp.dot(start_factor, updated, preferred_element_type=jnp.float32)
        left_total = lax.psum(local_left.astype(jnp.bfloat16), "tensor").astype(jnp.float32)
        left_diff = left_total - swap_left_side(left_total, pairing)
        gram_matrix = jnp.dot(left_diff, left_diff.T, precision=lax.Precision.HIGHEST)
        ortho_bf = orthonormal(gram_matrix, left_diff).astype(jnp.bfloat16)
        right_prod = lax.dot_general(
            ortho_bf, updated, (((1,), (1,)), ((), ())), preferred_element_type=jnp.float32
        )
        right_diff = (right_prod - swap_right_side(right_prod, pairing)).astype(jnp.bfloat16)
        change = lax.dot_general(
            right_diff, ortho_bf, (((0,), (0,)), ((), ())), preferred_element_type=jnp.float32
        )
        current = (updated.astype(jnp.float32) - 0.5 * change).astype(jnp.bfloat16)
    return current[None]


def solution(mesh):
    return jax.shard_map(
        per_device,
        mesh=mesh,
        in_specs=(
            P("replica", "tensor", None),
            P("replica", None, "tensor"),
            P("replica", None, "tensor"),
            P(None, None, "tensor"),
            P(),
        ),
        out_specs=P("replica", "tensor", None),
        check_vma=False,
    )
```

profile of v0, /device:TPU:0, one launch (start us, length us, event | category | flops | bytes accessed | tf_op | source)
XLA Modules:
  0.0 294.4 jit_solution(8720896719160545904)
XLA Ops:
  6.5 1.9 fusion.37
  8.4 0.0 all-gather.5.cloned.1.call-update
  8.4 0.0 copy-start.2
  8.4 0.0 all-reduce.3.cloned.1.call-start
  8.5 31.2 %all-gather.5.cloned.1.call-done = bf16[1,256,2048]{2,1,0:T(8,128)(2,1)} async-done(((bf16[1,256,512]{2,1,0:T(8,128)(2,1)}), bf16[1,256,2048]{2,1,0:T(8,128)(2,1)}) %all-gather.5.cloned.1.call-update) | async-done | bytes 1048592 | tf_op jit(solution)/shard_map/all_gather | solution.py:53
  39.6 12.2 %fusion = (bf16[2048,2048]{1,0:T(8,128)(2,1)S(1)}, f32[2048,2048]{1,0:T(8,128)}) fusion(bf16[1,2048,2048]{2,1,0:T(8,128)(2,1)} %param.8, bf16[1,256,2048]{2,1,0:T(8,128)(2,1)} %all-gather.5.cloned.1.call-done, bf16[1,512,2048]{2,1,0:T(8,128)(2,1)} %param.9), kind=kOutput, calls=%fused_computation.1 | convolution fusion | flops 2164260864 | bytes 35651584 | tf_op jit(solution)/shard_map/dot_general | solution.py:51
  51.8 3.4 %copy-done = bf16[2048,2048]{1,0:T(8,128)(2,1)} copy-done((bf16[2048,2048]{1,0:T(8,128)(2,1)}, bf16[2048,2048]{1,0:T(8,128)(2,1)S(1)}, u32[]{:S(2)}) %copy-start) | copy-done | bytes 8388632
  55.2 2.3 fusion.2
  57.5 0.0 all-reduce.3.cloned.1.call-update
  57.5 0.0 all-gather.7.cloned.1.call-start
  57.6 34.9 %all-reduce.3.cloned.1.call-done = bf16[64,2048]{1,0:T(8,128)(2,1)} async-done(((bf16[64,2048]{1,0:T(8,128)(2,1)}), bf16[64,2048]{1,0:T(8,128)(2,1)}) %all-reduce.3.cloned.1.call-update) | async-done | bytes 262160 | tf_op jit(solution)/shard_map/psum | solution.py:65
  92.5 0.6 fusion.38
  95.2 1.0 fusion.11
  96.2 1.5 collective-permute-start.1
  98.5 6.5 %collective-permute-done.1 = bf16[64,2048]{1,0:T(8,128)(2,1)S(1)} collective-permute-done((bf16[64,2048]{1,0:T(8,128)(2,1)S(1)}, bf16[64,2048]{1,0:T(8,128)(2,1)S(1)}, u32[]{:S(2)}, u32[]{:S(2)}) %collective-permute-start.1) | collective-permute-done | bytes 262176 | tf_op jit(solution)/shard_map/ppermute | solution.py:15
  105.0 1.0 fusion.13
  106.1 1.5 collective-permute-start.2
  107.6 6.4 %collective-permute-done.2 = bf16[64,2048]{1,0:T(8,128)(2,1)S(1)} collective-permute-done((bf16[64,2048]{1,0:T(8,128)(2,1)S(1)}, bf16[64,2048]{1,0:T(8,128)(2,1)S(1)}, u32[]{:S(2)}, u32[]{:S(2)}) %collective-permute-start.2) | collective-permute-done | bytes 262176 | tf_op jit(solution)/shard_map/ppermute | solution.py:15
  114.0 1.8 fusion.29
  115.8 0.1 copy.6
  115.9 5.8 %cholesky.44 = f32[64,64]{1,0:T(8,128)S(1)} custom-call(f32[64,64]{1,0:T(8,128)S(1)} %fusion.36), custom_call_target="Cholesky" | custom-call | tf_op jit(solution)/shard_map/jit(cholesky)/cholesky | solution.py:39
  121.8 0.7 compare_reduce_fusion.1
  122.5 0.7 fusion.31
  123.3 4.9 %custom-call.6 = f32[1,64,64]{1,2,0:T(8,128)S(1)} custom-call(f32[1,64,64]{2,1,0:T(8,128)S(1)} %fusion.31), custom_call_target="InvertDiagBlocksLowerTriangular" | custom-call | tf_op jit(solution)/shard_map/triangular_solve/custom-call.0 | solution.py:40
  128.2 1.7 convolution_convert_fusion.3
  129.8 6.0 %fusion.39 = (bf16[64,2048]{1,0:T(8,128)(2,1)S(1)}, f32[64,2048]{1,0:T(8,128)S(1)}) fusion(bf16[64,2048]{1,0:T(8,128)(2,1)S(1)} %convolution_convert_fusion.3, bf16[2048,2048]{1,0:T(8,128)(2,1)} %copy-done), kind=kOutput, calls=%fused_computation.69 | convolution fusion | flops 537001984 | bytes 9437184 | tf_op jit(solution)/shard_map/dot_general | solution.py:69
  135.9 0.1 collective-permute-start.3
  135.9 1.5 collective-permute-done.3
  137.5 1.5 collective-permute-start.4
  139.1 0.0 all-gather.7.cloned.1.call-update
  139.1 0.2 all-reduce.5.cloned.1.call-start
  139.3 6.6 %collective-permute-done.4 = bf16[64,2048]{1,0:T(8,128)(2,1)S(1)} collective-permute-done((bf16[64,2048]{1,0:T(8,128)(2,1)S(1)}, bf16[64,2048]{1,0:T(8,128)(2,1)S(1)}, u32[]{:S(2)}, u32[]{:S(2)}) %collective-permute-start.4) | collective-permute-done | bytes 262176 | tf_op jit(solution)/shard_map/ppermute | solution.py:15
  145.9 0.1 fusion.16
  146.0 0.0 copy-start.1
  146.0 1.5 collective-permute-start.5
  147.6 6.0 %collective-permute-done.5 = bf16[64,2048]{1,0:T(8,128)(2,1)S(1)} collective-permute-done((bf16[64,2048]{1,0:T(8,128)(2,1)S(1)}, bf16[64,2048]{1,0:T(8,128)(2,1)S(1)}, u32[]{:S(2)}, u32[]{:S(2)}) %collective-permute-start.5) | collective-permute-done | bytes 262176 | tf_op jit(solution)/shard_map/ppermute | solution.py:15
  153.6 6.9 %subtract_convert_fusion.2 = bf16[2048,2048]{1,0:T(8,128)(2,1)} fusion(bf16[2048,2048]{1,0:T(8,128)(2,1)} %copy-done, bf16[64,2048]{1,0:T(8,128)(2,1)S(1)} %convolution_convert_fusion.3, f32[64,2048]{1,0:T(8,128)S(1)} %get-tuple-element.14, bf16[64,2048]{1,0:T(8,128)(2,1)S(1)} %collective-permute-done.5, bf16[64,2048]{1,0:T(8,128)(2,1)S(1)} %collective-permute-done.3, ...), kind=kOutput, calls=%fused_computation.4 | convolution fusion | flops 554696704 | bytes 18350084 | tf_op jit(solution)/shard_map/dot_general | solution.py:73
  160.5 5.7 %all-gather.7.cloned.1.call-done = bf16[1,256,2048]{2,1,0:T(8,128)(2,1)} async-done(((bf16[1,256,512]{2,1,0:T(8,128)(2,1)}), bf16[1,256,2048]{2,1,0:T(8,128)(2,1)}) %all-gather.7.cloned.1.call-update) | async-done | bytes 1048592 | tf_op jit(solution)/shard_map/all_gather | solution.py:53
  166.2 14.0 %subtract_convert_fusion.1 = bf16[2048,2048]{1,0:T(8,128)(2,1)} fusion(f32[2048,2048]{1,0:T(8,128)} %get-tuple-element.12, bf16[2048,2048]{1,0:T(8,128)(2,1)} %subtract_convert_fusion.2, bf16[1,256,2048]{2,1,0:T(8,128)(2,1)} %all-gather.7.cloned.1.call-done, bf16[1,512,2048]{2,1,0:T(8,128)(2,1)S(1)} %copy-done.1), kind=kOutput, calls=%fused_computation.3 | convolution fusion | flops 2172649472 | bytes 35651584 | tf_op jit(solution)/shard_map/dot_general | solution.py:51
  180.2 5.6 %fusion.3 = bf16[64,2048]{1,0:T(8,128)(2,1)} fusion(bf16[2048,2048]{1,0:T(8,128)(2,1)} %subtract_convert_fusion.1, bf16[2,64,2048]{2,1,0:T(8,128)(2,1)S(1)} %copy-done.3), kind=kOutput, calls=%fused_computation.11 | convolution fusion | flops 537001984 | bytes 8912896 | tf_op jit(solution)/shard_map/dot_general | solution.py:64
  185.8 0.0 all-reduce.5.cloned.1.call-update
  185.8 35.1 %all-reduce.5.cloned.1.call-done = bf16[64,2048]{1,0:T(8,128)(2,1)} async-done(((bf16[64,2048]{1,0:T(8,128)(2,1)}), bf16[64,2048]{1,0:T(8,128)(2,1)}) %all-reduce.5.cloned.1.call-update) | async-done | bytes 262160 | tf_op jit(solution)/shard_map/psum | solution.py:65
  222.8 1.0 fusion.12
  223.8 1.5 collective-permute-start.7
  226.0 6.6 %collective-permute-done.7 = bf16[64,2048]{1,0:T(8,128)(2,1)S(1)} collective-permute-done((bf16[64,2048]{1,0:T(8,128)(2,1)S(1)}, bf16[64,2048]{1,0:T(8,128)(2,1)S(1)}, u32[]{:S(2)}, u32[]{:S(2)}) %collective-permute-start.7) | collective-permute-done | bytes 262176 | tf_op jit(solution)/shard_map/ppermute | solution.py:15
  232.6 1.0 fusion.14
  233.7 1.5 collective-permute-start.8
  235.2 6.4 %collective-permute-done.8 = bf16[64,2048]{1,0:T(8,128)(2,1)S(1)} collective-permute-done((bf16[64,2048]{1,0:T(8,128)(2,1)S(1)}, bf16[64,2048]{1,0:T(8,128)(2,1)S(1)}, u32[]{:S(2)}, u32[]{:S(2)}) %collective-permute-start.8) | collective-permute-done | bytes 262176 | tf_op jit(solution)/shard_map/ppermute | solution.py:15
  241.6 1.8 fusion.30
  243.5 0.1 copy.7
  243.5 5.8 %cholesky.55 = f32[64,64]{1,0:T(8,128)S(1)} custom-call(f32[64,64]{1,0:T(8,128)S(1)} %fusion.34), custom_call_target="Cholesky" | custom-call | tf_op jit(solution)/shard_map/jit(cholesky)/cholesky | solution.py:39
  249.4 0.6 compare_reduce_fusion
  250.1 0.6 fusion.32
  250.6 4.9 %custom-call.7 = f32[1,64,64]{1,2,0:T(8,128)S(1)} custom-call(f32[1,64,64]{2,1,0:T(8,128)S(1)} %fusion.32), custom_call_target="InvertDiagBlocksLowerTriangular" | custom-call | tf_op jit(solution)/shard_map/triangular_solve/custom-call.0 | solution.py:40
  255.5 1.7 convolution_convert_fusion.2
  257.2 6.0 %fusion.40 = (bf16[64,2048]{1,0:T(8,128)(2,1)S(1)}, f32[64,2048]{1,0:T(8,128)S(1)}) fusion(bf16[64,2048]{1,0:T(8,128)(2,1)S(1)} %convolution_convert_fusion.2, bf16[2048,2048]{1,0:T(8,128)(2,1)} %subtract_convert_fusion.1), kind=kOutput, calls=%fused_computation.70 | convolution fusion | flops 537001984 | bytes 9437184 | tf_op jit(solution)/shard_map/dot_general | solution.py:69
  263.3 0.1 collective-permute-start.9
  263.3 1.5 collective-permute-done.9
  264.9 1.5 collective-permute-start.10
  266.4 6.9 %collective-permute-done.10 = bf16[64,2048]{1,0:T(8,128)(2,1)S(1)} collective-permute-done((bf16[64,2048]{1,0:T(8,128)(2,1)S(1)}, bf16[64,2048]{1,0:T(8,128)(2,1)S(1)}, u32[]{:S(2)}, u32[]{:S(2)}) %collective-permute-start.10) | collective-permute-done | bytes 262176 | tf_op jit(solution)/shard_map/ppermute | solution.py:15
  273.3 0.1 fusion.18
  273.4 1.5 collective-permute-start.11
  275.0 6.0 %collective-permute-done.11 = bf16[64,2048]{1,0:T(8,128)(2,1)S(1)} collective-permute-done((bf16[64,2048]{1,0:T(8,128)(2,1)S(1)}, bf16[64,2048]{1,0:T(8,128)(2,1)S(1)}, u32[]{:S(2)}, u32[]{:S(2)}) %collective-permute-start.11) | collective-permute-done | bytes 262176 | tf_op jit(solution)/shard_map/ppermute | solution.py:15
  281.0 6.9 %fusion.1 = bf16[1,2048,2048]{2,1,0:T(8,128)(2,1)} fusion(bf16[64,2048]{1,0:T(8,128)(2,1)S(1)} %convolution_convert_fusion.2, bf16[2048,2048]{1,0:T(8,128)(2,1)} %subtract_convert_fusion.1, f32[64,2048]{1,0:T(8,128)S(1)} %get-tuple-element.16, bf16[64,2048]{1,0:T(8,128)(2,1)S(1)} %collective-permute-done.11, ...), kind=kOutput, calls=%fused_computation.5 | convolution fusion | flops 554696704 | bytes 18350084 | tf_op jit(solution)/shard_map/dot_general | solution.py:73
  (18 shorter events, 0.2 us)
Async XLA Ops:
  6.5 33.1 %all-gather.5.cloned.1.call-start = ((), (), s32[]{:S(2)}) async-start(), calls=%async_computation.2 | async-start | bytes 1310720 | tf_op jit(solution)/shard_map/all_gather | solution.py:53
  8.4 46.8 %copy-start.2 = (bf16[2,64,2048]{2,1,0:T(8,128)(2,1)S(1)}, bf16[2,64,2048]{2,1,0:T(8,128)(2,1)}, u32[]{:S(2)}) copy-start(bf16[2,64,2048]{2,1,0:T(8,128)(2,1)} %param.11) | copy-start | bytes 1572868
  8.4 84.1 %all-reduce.3.cloned.1.call-start = ((), (), s32[]{:S(2)}) async-start(), calls=%async_computation | async-start | bytes 524288 | tf_op jit(solution)/shard_map/psum | solution.py:65
  51.8 3.4 %copy-start = (bf16[2048,2048]{1,0:T(8,128)(2,1)}, bf16[2048,2048]{1,0:T(8,128)(2,1)S(1)}, u32[]{:S(2)}) copy-start(bf16[2048,2048]{1,0:T(8,128)(2,1)S(1)} %get-tuple-element.11) | copy-start | bytes 25165828
  51.8 40.6 %copy-start.4 = (s32[2]{0:T(128)S(1)}, s32[2]{0:T(128)}, u32[]{:S(2)}) copy-start(s32[2]{0:T(128)} %param.12) | copy-start | bytes 28
  57.5 108.6 %all-gather.7.cloned.1.call-start = ((), (), s32[]{:S(2)}) async-start(), calls=%async_computation.3 | async-start | bytes 1310720 | tf_op jit(solution)/shard_map/all_gather | solution.py:53
  92.5 2.7 collective-permute-start
  96.2 8.8 %collective-permute-start.1 = (bf16[64,2048]{1,0:T(8,128)(2,1)S(1)}, bf16[64,2048]{1,0:T(8,128)(2,1)S(1)}, u32[]{:S(2)}, u32[]{:S(2)}) collective-permute-start(bf16[64,2048]{1,0:T(8,128)(2,1)S(1)} %fusion.11), channel_id=1, source_target_pairs={{0,8},{4,12},{8,0},{12,4},{16,24},{20,28},{24,16},{28,20},{1,9},{5... | collective-permute-start | bytes 786440 | tf_op jit(solution)/shard_map/ppermute | solution.py:15
  106.1 7.9 %collective-permute-start.2 = (bf16[64,2048]{1,0:T(8,128)(2,1)S(1)}, bf16[64,2048]{1,0:T(8,128)(2,1)S(1)}, u32[]{:S(2)}, u32[]{:S(2)}) collective-permute-start(bf16[64,2048]{1,0:T(8,128)(2,1)S(1)} %fusion.13), channel_id=1, source_target_pairs={{0,16},{4,20},{8,24},{12,28},{16,0},{20,4},{24,8},{28,12},{1,17},{... | collective-permute-start | bytes 786440 | tf_op jit(solution)/shard_map/ppermute | solution.py:15
  135.9 1.6 collective-permute-start.3
  137.5 8.4 %collective-permute-start.4 = (bf16[64,2048]{1,0:T(8,128)(2,1)S(1)}, bf16[64,2048]{1,0:T(8,128)(2,1)S(1)}, u32[]{:S(2)}, u32[]{:S(2)}) collective-permute-start(bf16[64,2048]{1,0:T(8,128)(2,1)S(1)} %fusion.15), channel_id=1, source_target_pairs={{0,8},{4,12},{8,0},{12,4},{16,24},{20,28},{24,16},{28,20},{1,9},{5... | collective-permute-start | bytes 786440 | tf_op jit(solution)/shard_map/ppermute | solution.py:15
  139.1 81.9 %all-reduce.5.cloned.1.call-start = ((), (), s32[]{:S(2)}) async-start(), calls=%async_computation.1 | async-start | bytes 524288 | tf_op jit(solution)/shard_map/psum | solution.py:65
  146.0 20.2 %copy-start.1 = (bf16[1,512,2048]{2,1,0:T(8,128)(2,1)S(1)}, bf16[1,512,2048]{2,1,0:T(8,128)(2,1)}, u32[]{:S(2)}) copy-start(bf16[1,512,2048]{2,1,0:T(8,128)(2,1)} %param.9) | copy-start | bytes 6291460
  146.0 7.6 %collective-permute-start.5 = (bf16[64,2048]{1,0:T(8,128)(2,1)S(1)}, bf16[64,2048]{1,0:T(8,128)(2,1)S(1)}, u32[]{:S(2)}, u32[]{:S(2)}) collective-permute-start(bf16[64,2048]{1,0:T(8,128)(2,1)S(1)} %fusion.16), channel_id=1, source_target_pairs={{0,16},{4,20},{8,24},{12,28},{16,0},{20,4},{24,8},{28,12},{1,17},{... | collective-permute-start | bytes 786440 | tf_op jit(solution)/shard_map/ppermute | solution.py:15
  166.2 14.0 %copy-start.3 = (bf16[2,64,2048]{2,1,0:T(8,128)(2,1)S(1)}, bf16[2,64,2048]{2,1,0:T(8,128)(2,1)}, u32[]{:S(2)}) copy-start(bf16[2,64,2048]{2,1,0:T(8,128)(2,1)} %param.11) | copy-start | bytes 1572868
  221.0 1.9 collective-permute-start.6
  223.8 8.8 %collective-permute-start.7 = (bf16[64,2048]{1,0:T(8,128)(2,1)S(1)}, bf16[64,2048]{1,0:T(8,128)(2,1)S(1)}, u32[]{:S(2)}, u32[]{:S(2)}) collective-permute-start(bf16[64,2048]{1,0:T(8,128)(2,1)S(1)} %fusion.12), channel_id=1, source_target_pairs={{0,8},{4,12},{8,0},{12,4},{16,24},{20,28},{24,16},{28,20},{1,9},{5... | collective-permute-start | bytes 786440 | tf_op jit(solution)/shard_map/ppermute | solution.py:15
  233.7 7.9 %collective-permute-start.8 = (bf16[64,2048]{1,0:T(8,128)(2,1)S(1)}, bf16[64,2048]{1,0:T(8,128)(2,1)S(1)}, u32[]{:S(2)}, u32[]{:S(2)}) collective-permute-start(bf16[64,2048]{1,0:T(8,128)(2,1)S(1)} %fusion.14), channel_id=1, source_target_pairs={{0,16},{4,20},{8,24},{12,28},{16,0},{20,4},{24,8},{28,12},{1,17},{... | collective-permute-start | bytes 786440 | tf_op jit(solution)/shard_map/ppermute | solution.py:15
  263.3 1.6 collective-permute-start.9
  264.9 8.4 %collective-permute-start.10 = (bf16[64,2048]{1,0:T(8,128)(2,1)S(1)}, bf16[64,2048]{1,0:T(8,128)(2,1)S(1)}, u32[]{:S(2)}, u32[]{:S(2)}) collective-permute-start(bf16[64,2048]{1,0:T(8,128)(2,1)S(1)} %fusion.17), channel_id=1, source_target_pairs={{0,8},{4,12},{8,0},{12,4},{16,24},{20,28},{24,16},{28,20},{1,9},{5... | collective-permute-start | bytes 786440 | tf_op jit(solution)/shard_map/ppermute | solution.py:15
  273.4 7.6 %collective-permute-start.11 = (bf16[64,2048]{1,0:T(8,128)(2,1)S(1)}, bf16[64,2048]{1,0:T(8,128)(2,1)S(1)}, u32[]{:S(2)}, u32[]{:S(2)}) collective-permute-start(bf16[64,2048]{1,0:T(8,128)(2,1)S(1)} %fusion.18), channel_id=1, source_target_pairs={{0,16},{4,20},{8,24},{12,28},{16,0},{20,4},{24,8},{28,12},{1,17},{... | collective-permute-start | bytes 786440 | tf_op jit(solution)/shard_map/ppermute | solution.py:15
Sparse Core Ops, SparseCore 0:
  8.9 30.6 all-gather.4
  57.7 34.7 all-reduce.2
  139.2 26.9 all-gather.6
  186.0 34.9 all-reduce.4
where the time goes:
time: 295 us; the launch traced here: 294 us
  waiting for transfers between devices  161 us (55%)
  matrix products  67 us (23%)
  other arithmetic  28.6 us (10%)
  between operations  18.6 us (6%)
  starting transfers between devices  12.7 us (4%)
  local copies, waits for them, and re-layouts  6.03 us (2%)
    psum x2, waiting for transfers between devices, per_device(): lax.psum(local_left.astype(jnp.bfloat16), 'tensor').astype(jnp.float32)  70 us
    ppermute x12, waiting for transfers between devices, from_partner(): return lax.ppermute(value, axis, pairs)  54.5 us
    all_gather x2, waiting for transfers between devices, per_device(): lax.all_gather(grads_step, 'tensor', axis=1, tiled=True)  36.8 us
    dot_general x2, matrix products, per_device(): lax.dot_general(hidden_step, lax.all_gather(grads_step, 'tensor', axis=1,...  26.2 us
    dot_general x2, matrix products, per_device(): lax.dot_general(right_diff, ortho_bf, (((0,), (0,)), ((), ())), preferred...  13.8 us
    another operation x6, other arithmetic, orthonormal(): lower_factor = jnp.linalg.cholesky(gram_matrix)  13.1 us
    ppermute x12, starting transfers between devices, from_partner(): return lax.ppermute(value, axis, pairs)  12.4 us
    dot_general x2, matrix products, per_device(): lax.dot_general(ortho_bf, updated, (((1,), (1,)), ((), ())), preferred_el...  12.1 us
  transfers between devices with their start and end apart: 16, of which 14 were waited for; matrix products, arithmetic and copies ran while one was open for 3% of the time, Pallas kernels for 0%

commit v1 on v0

--- a/solution.py
+++ b/solution.py
@@ -1,3 +1,4 @@
+import functools
 import jax
 import jax.numpy as jnp
 from jax import lax
@@ -7,6 +8,13 @@
 TOK = 256
 learn_rate = 0.1
 momentum_decay = 0.9
+
+
+def _match_groups(incoming_x, dev_axis):
+    return jnp.sum(jax.lax.all_gather(incoming_x, dev_axis), axis=0)
+
+
+watch_the_targets = functools.partial(_match_groups, dev_axis="tensor")
 
 
 def from_partner(value, axis, bit):
@@ -62,7 +70,7 @@
         start_factor = factor_start[step_index]
         pairing = matching[step_index]
         local_left = jnp.dot(start_factor, updated, preferred_element_type=jnp.float32)
-        left_total = lax.psum(local_left.astype(jnp.bfloat16), "tensor").astype(jnp.float32)
+        left_total = watch_the_targets(local_left.astype(jnp.bfloat16)).astype(jnp.float32)
         left_diff = left_total - swap_left_side(left_total, pairing)
         gram_matrix = jnp.dot(left_diff, left_diff.T, precision=lax.Precision.HIGHEST)
         ortho_bf = orthonormal(gram_matrix, left_diff).astype(jnp.bfloat16)

time: 295 us -> 274 us (0.929)
  waiting for transfers between devices: 161 us -> 146 us
  matrix products: 67 us -> 63 us
    psum x2 -> x0, waiting for transfers between devices: 70 us -> none  [per_device(): lax.psum(local_left.astype(jnp.bfloat16), 'tensor').astype(jnp.float32)]
    all_gather x0 -> x2, waiting for transfers between devices: none -> 55 us  [_match_groups(): return jnp.sum(jax.lax.all_gather(incoming_x, dev_axis), axis=0)]
    convert_element_type x4, other arithmetic: 4.13 us -> 0.33 us  [swap_left_side(): payload.astype(jnp.bfloat16)]
where the time goes in v1:
time: 274 us
  waiting for transfers between devices  146 us (53%)
  matrix products  63 us (23%)
  other arithmetic  27.6 us (10%)
  between operations  18.4 us (7%)
  starting transfers between devices  12.9 us (5%)
  local copies, waits for them, and re-layouts  6.03 us (2%)
    all_gather x2, waiting for transfers between devices, _match_groups(): return jnp.sum(jax.lax.all_gather(incoming_x, dev_axis), axis=0)  55 us
    ppermute x12, waiting for transfers between devices, from_partner(): return lax.ppermute(value, axis, pairs)  54.5 us
    all_gather x2, waiting for transfers between devices, per_device(): lax.all_gather(grads_step, 'tensor', axis=1, tiled=True)  36.4 us
    dot_general x2, matrix products, per_device(): lax.dot_general(hidden_step, lax.all_gather(grads_step, 'tensor', axis=1,...  26.2 us
    dot_general x2, matrix products, per_device(): lax.dot_general(right_diff, ortho_bf, (((0,), (0,)), ((), ())), preferred...  13.8 us
    another operation x6, other arithmetic, orthonormal(): lower_factor = jnp.linalg.cholesky(gram_matrix)  13.1 us
    ppermute x12, starting transfers between devices, from_partner(): return lax.ppermute(value, axis, pairs)  12.6 us
    dot_general x2, matrix products, per_device(): lax.dot_general(ortho_bf, updated, (((1,), (1,)), ((), ())), preferred_el...  12.1 us
  transfers between devices with their start and end apart: 16, of which 14 were waited for; matrix products, arithmetic and copies ran while one was open for 3% of the time, Pallas kernels for 0%

profile of v1, /device:TPU:0, one launch (start us, length us, event | category | flops | bytes accessed | tf_op | source)
XLA Modules:
  0.0 273.8 jit_solution(3955755211666089733)
XLA Ops:
  6.5 1.9 fusion.37
  8.4 0.0 all-gather.9.cloned.1.call-update
  8.4 0.0 all-gather.11.cloned.1.call-start
  8.5 31.2 %all-gather.9.cloned.1.call-done = bf16[1,256,2048]{2,1,0:T(8,128)(2,1)} async-done(((bf16[1,256,512]{2,1,0:T(8,128)(2,1)}), bf16[1,256,2048]{2,1,0:T(8,128)(2,1)}) %all-gather.9.cloned.1.call-update) | async-done | bytes 1048592 | tf_op jit(solution)/shard_map/all_gather | solution.py:61
  39.6 12.2 %fusion = (bf16[2048,2048]{1,0:T(8,128)(2,1)S(1)}, f32[2048,2048]{1,0:T(8,128)}) fusion(bf16[1,2048,2048]{2,1,0:T(8,128)(2,1)} %param.8, bf16[1,256,2048]{2,1,0:T(8,128)(2,1)} %all-gather.9.cloned.1.call-done, bf16[1,512,2048]{2,1,0:T(8,128)(2,1)} %param.9), kind=kOutput, calls=%fused_computation.1 | convolution fusion | flops 2164260864 | bytes 35651584 | tf_op jit(solution)/shard_map/dot_general | solution.py:59
  51.8 3.4 %copy-done = bf16[2048,2048]{1,0:T(8,128)(2,1)} copy-done((bf16[2048,2048]{1,0:T(8,128)(2,1)}, bf16[2048,2048]{1,0:T(8,128)(2,1)S(1)}, u32[]{:S(2)}) %copy-start) | copy-done | bytes 8388632
  55.2 2.3 fusion.2
  57.5 0.0 all-gather.11.cloned.1.call-update
  57.6 0.0 all-gather.13.cloned.1.call-start
  57.6 27.5 %all-gather.11.cloned.1.call-done = bf16[256,2048]{1,0:T(8,128)(2,1)} async-done(((bf16[64,2048]{1,0:T(8,128)(2,1)}), bf16[256,2048]{1,0:T(8,128)(2,1)}) %all-gather.11.cloned.1.call-update) | async-done | bytes 1048592 | tf_op jit(solution)/shard_map/all_gather | solution.py:14
  85.1 1.4 reduce_sum.24
  86.5 0.1 collective-permute-start
  86.6 0.6 fusion.38
  89.1 0.1 fusion.11
  89.2 1.5 collective-permute-start.1
  91.4 6.6 %collective-permute-done.1 = bf16[64,2048]{1,0:T(8,128)(2,1)S(1)} collective-permute-done((bf16[64,2048]{1,0:T(8,128)(2,1)S(1)}, bf16[64,2048]{1,0:T(8,128)(2,1)S(1)}, u32[]{:S(2)}, u32[]{:S(2)}) %collective-permute-start.1) | collective-permute-done | bytes 262176 | tf_op jit(solution)/shard_map/ppermute | solution.py:23
  97.9 0.1 fusion.13
  98.0 1.5 collective-permute-start.2
  99.6 6.4 %collective-permute-done.2 = bf16[64,2048]{1,0:T(8,128)(2,1)S(1)} collective-permute-done((bf16[64,2048]{1,0:T(8,128)(2,1)S(1)}, bf16[64,2048]{1,0:T(8,128)(2,1)S(1)}, u32[]{:S(2)}, u32[]{:S(2)}) %collective-permute-start.2) | collective-permute-done | bytes 262176 | tf_op jit(solution)/shard_map/ppermute | solution.py:23
  105.9 0.8 fusion.29
  106.7 0.1 copy.6
  106.8 5.8 %cholesky.44 = f32[64,64]{1,0:T(8,128)S(1)} custom-call(f32[64,64]{1,0:T(8,128)S(1)} %fusion.36), custom_call_target="Cholesky" | custom-call | tf_op jit(solution)/shard_map/jit(cholesky)/cholesky | solution.py:47
  112.7 0.7 compare_reduce_fusion.1
  113.4 0.6 fusion.31
  114.0 4.9 %custom-call.6 = f32[1,64,64]{1,2,0:T(8,128)S(1)} custom-call(f32[1,64,64]{2,1,0:T(8,128)S(1)} %fusion.31), custom_call_target="InvertDiagBlocksLowerTriangular" | custom-call | tf_op jit(solution)/shard_map/triangular_solve/custom-call.0 | solution.py:48
  118.9 0.7 convolution_convert_fusion.3
  119.7 6.0 %fusion.39 = (bf16[64,2048]{1,0:T(8,128)(2,1)S(1)}, f32[64,2048]{1,0:T(8,128)S(1)}) fusion(bf16[64,2048]{1,0:T(8,128)(2,1)S(1)} %convolution_convert_fusion.3, bf16[2048,2048]{1,0:T(8,128)(2,1)} %copy-done), kind=kOutput, calls=%fused_computation.69 | convolution fusion | flops 537001984 | bytes 9437184 | tf_op jit(solution)/shard_map/dot_general | solution.py:77
  125.7 0.1 collective-permute-start.3
  125.8 1.5 collective-permute-done.3
  127.3 1.5 collective-permute-start.4
  128.9 0.2 all-gather.15.cloned.1.call-start
  129.1 6.6 %collective-permute-done.4 = bf16[64,2048]{1,0:T(8,128)(2,1)S(1)} collective-permute-done((bf16[64,2048]{1,0:T(8,128)(2,1)S(1)}, bf16[64,2048]{1,0:T(8,128)(2,1)S(1)}, u32[]{:S(2)}, u32[]{:S(2)}) %collective-permute-start.4) | collective-permute-done | bytes 262176 | tf_op jit(solution)/shard_map/ppermute | solution.py:23
  135.8 0.1 fusion.16
  135.9 1.5 collective-permute-start.5
  137.4 6.0 %collective-permute-done.5 = bf16[64,2048]{1,0:T(8,128)(2,1)S(1)} collective-permute-done((bf16[64,2048]{1,0:T(8,128)(2,1)S(1)}, bf16[64,2048]{1,0:T(8,128)(2,1)S(1)}, u32[]{:S(2)}, u32[]{:S(2)}) %collective-permute-start.5) | collective-permute-done | bytes 262176 | tf_op jit(solution)/shard_map/ppermute | solution.py:23
  143.4 6.9 %subtract_convert_fusion.2 = bf16[2048,2048]{1,0:T(8,128)(2,1)} fusion(bf16[2048,2048]{1,0:T(8,128)(2,1)} %copy-done, bf16[64,2048]{1,0:T(8,128)(2,1)S(1)} %convolution_convert_fusion.3, f32[64,2048]{1,0:T(8,128)S(1)} %get-tuple-element.14, bf16[64,2048]{1,0:T(8,128)(2,1)S(1)} %collective-permute-done.5, bf16[64,2048]{1,0:T(8,128)(2,1)S(1)} %collective-permute-done.3, ...), kind=kOutput, calls=%fused_computation.4 | convolution fusion | flops 554696704 | bytes 18350084 | tf_op jit(solution)/shard_map/dot_general | solution.py:81
  150.3 5.2 %all-gather.13.cloned.1.call-done = bf16[1,256,2048]{2,1,0:T(8,128)(2,1)} async-done(((bf16[1,256,512]{2,1,0:T(8,128)(2,1)}), bf16[1,256,2048]{2,1,0:T(8,128)(2,1)}) %all-gather.13.cloned.1.call-update) | async-done | bytes 1048592 | tf_op jit(solution)/shard_map/all_gather | solution.py:61
  155.5 14.0 %subtract_convert_fusion.1 = bf16[2048,2048]{1,0:T(8,128)(2,1)} fusion(f32[2048,2048]{1,0:T(8,128)} %get-tuple-element.12, bf16[2048,2048]{1,0:T(8,128)(2,1)} %subtract_convert_fusion.2, bf16[1,256,2048]{2,1,0:T(8,128)(2,1)} %all-gather.13.cloned.1.call-done, bf16[1,512,2048]{2,1,0:T(8,128)(2,1)S(1)} %copy-done.1), kind=kOutput, calls=%fused_computation.3 | convolution fusion | flops 2172649472 | bytes 35651584 | tf_op jit(solution)/shard_map/dot_general | solution.py:59
  169.5 5.7 %fusion.3 = bf16[64,2048]{1,0:T(8,128)(2,1)} fusion(bf16[2048,2048]{1,0:T(8,128)(2,1)} %subtract_convert_fusion.1, bf16[2,64,2048]{2,1,0:T(8,128)(2,1)S(1)} %copy-done.3), kind=kOutput, calls=%fused_computation.11 | convolution fusion | flops 537001984 | bytes 8912896 | tf_op jit(solution)/shard_map/dot_general | solution.py:72
  175.2 27.5 %all-gather.15.cloned.1.call-done = bf16[256,2048]{1,0:T(8,128)(2,1)} async-done(((bf16[64,2048]{1,0:T(8,128)(2,1)}), bf16[256,2048]{1,0:T(8,128)(2,1)}) %all-gather.15.cloned.1.call-update) | async-done | bytes 1048592 | tf_op jit(solution)/shard_map/all_gather | solution.py:14
  202.7 1.4 reduce_sum.25
  204.1 0.1 collective-permute-start.6
  206.0 0.1 fusion.12
  206.1 1.5 collective-permute-start.7
  208.3 6.6 %collective-permute-done.7 = bf16[64,2048]{1,0:T(8,128)(2,1)S(1)} collective-permute-done((bf16[64,2048]{1,0:T(8,128)(2,1)S(1)}, bf16[64,2048]{1,0:T(8,128)(2,1)S(1)}, u32[]{:S(2)}, u32[]{:S(2)}) %collective-permute-start.7) | collective-permute-done | bytes 262176 | tf_op jit(solution)/shard_map/ppermute | solution.py:23
  214.9 0.1 fusion.14
  215.0 1.5 collective-permute-start.8
  216.5 6.4 %collective-permute-done.8 = bf16[64,2048]{1,0:T(8,128)(2,1)S(1)} collective-permute-done((bf16[64,2048]{1,0:T(8,128)(2,1)S(1)}, bf16[64,2048]{1,0:T(8,128)(2,1)S(1)}, u32[]{:S(2)}, u32[]{:S(2)}) %collective-permute-start.8) | collective-permute-done | bytes 262176 | tf_op jit(solution)/shard_map/ppermute | solution.py:23
  222.9 0.8 fusion.30
  223.7 0.1 copy.7
  223.8 5.8 %cholesky.55 = f32[64,64]{1,0:T(8,128)S(1)} custom-call(f32[64,64]{1,0:T(8,128)S(1)} %fusion.34), custom_call_target="Cholesky" | custom-call | tf_op jit(solution)/shard_map/jit(cholesky)/cholesky | solution.py:47
  229.6 0.7 compare_reduce_fusion
  230.3 0.6 fusion.32
  231.0 4.9 %custom-call.7 = f32[1,64,64]{1,2,0:T(8,128)S(1)} custom-call(f32[1,64,64]{2,1,0:T(8,128)S(1)} %fusion.32), custom_call_target="InvertDiagBlocksLowerTriangular" | custom-call | tf_op jit(solution)/shard_map/triangular_solve/custom-call.0 | solution.py:48
  235.9 0.7 convolution_convert_fusion.2
  236.6 6.0 %fusion.40 = (bf16[64,2048]{1,0:T(8,128)(2,1)S(1)}, f32[64,2048]{1,0:T(8,128)S(1)}) fusion(bf16[64,2048]{1,0:T(8,128)(2,1)S(1)} %convolution_convert_fusion.2, bf16[2048,2048]{1,0:T(8,128)(2,1)} %subtract_convert_fusion.1), kind=kOutput, calls=%fused_computation.70 | convolution fusion | flops 537001984 | bytes 9437184 | tf_op jit(solution)/shard_map/dot_general | solution.py:77
  242.6 0.1 collective-permute-start.9
  242.7 1.5 collective-permute-done.9
  244.3 1.5 collective-permute-start.10
  245.8 6.9 %collective-permute-done.10 = bf16[64,2048]{1,0:T(8,128)(2,1)S(1)} collective-permute-done((bf16[64,2048]{1,0:T(8,128)(2,1)S(1)}, bf16[64,2048]{1,0:T(8,128)(2,1)S(1)}, u32[]{:S(2)}, u32[]{:S(2)}) %collective-permute-start.10) | collective-permute-done | bytes 262176 | tf_op jit(solution)/shard_map/ppermute | solution.py:23
  252.7 0.1 fusion.18
  252.8 1.5 collective-permute-start.11
  254.3 6.0 %collective-permute-done.11 = bf16[64,2048]{1,0:T(8,128)(2,1)S(1)} collective-permute-done((bf16[64,2048]{1,0:T(8,128)(2,1)S(1)}, bf16[64,2048]{1,0:T(8,128)(2,1)S(1)}, u32[]{:S(2)}, u32[]{:S(2)}) %collective-permute-start.11) | collective-permute-done | bytes 262176 | tf_op jit(solution)/shard_map/ppermute | solution.py:23
  260.3 6.9 %fusion.1 = bf16[1,2048,2048]{2,1,0:T(8,128)(2,1)} fusion(bf16[64,2048]{1,0:T(8,128)(2,1)S(1)} %convolution_convert_fusion.2, bf16[2048,2048]{1,0:T(8,128)(2,1)} %subtract_convert_fusion.1, f32[64,2048]{1,0:T(8,128)S(1)} %get-tuple-element.16, bf16[64,2048]{1,0:T(8,128)(2,1)S(1)} %collective-permute-done.11, ...), kind=kOutput, calls=%fused_computation.5 | convolution fusion | flops 554696704 | bytes 18350084 | tf_op jit(solution)/shard_map/dot_general | solution.py:81
  (20 shorter events, 0.2 us)
Async XLA Ops:
  6.5 33.1 %all-gather.9.cloned.1.call-start = ((), (), s32[]{:S(2)}) async-start(), calls=%async_computation | async-start | bytes 1310720 | tf_op jit(solution)/shard_map/all_gather | solution.py:61
  8.4 46.8 %copy-start.2 = (bf16[2,64,2048]{2,1,0:T(8,128)(2,1)S(1)}, bf16[2,64,2048]{2,1,0:T(8,128)(2,1)}, u32[]{:S(2)}) copy-start(bf16[2,64,2048]{2,1,0:T(8,128)(2,1)} %param.11) | copy-start | bytes 1572868
  8.4 76.7 %all-gather.11.cloned.1.call-start = ((), (), s32[]{:S(2)}) async-start(), calls=%async_computation.1 | async-start | bytes 1310720 | tf_op jit(solution)/shard_map/all_gather | solution.py:14
  51.8 3.4 %copy-start = (bf16[2048,2048]{1,0:T(8,128)(2,1)}, bf16[2048,2048]{1,0:T(8,128)(2,1)S(1)}, u32[]{:S(2)}) copy-start(bf16[2048,2048]{1,0:T(8,128)(2,1)S(1)} %get-tuple-element.11) | copy-start | bytes 25165828
  55.2 31.3 %copy-start.4 = (s32[2]{0:T(128)S(1)}, s32[2]{0:T(128)}, u32[]{:S(2)}) copy-start(s32[2]{0:T(128)} %param.12) | copy-start | bytes 28
  57.6 97.9 %all-gather.13.cloned.1.call-start = ((), (), s32[]{:S(2)}) async-start(), calls=%async_computation.2 | async-start | bytes 1310720 | tf_op jit(solution)/shard_map/all_gather | solution.py:61
  86.5 2.6 collective-permute-start
  89.2 8.8 %collective-permute-start.1 = (bf16[64,2048]{1,0:T(8,128)(2,1)S(1)}, bf16[64,2048]{1,0:T(8,128)(2,1)S(1)}, u32[]{:S(2)}, u32[]{:S(2)}) collective-permute-start(bf16[64,2048]{1,0:T(8,128)(2,1)S(1)} %fusion.11), channel_id=1, source_target_pairs={{0,8},{4,12},{8,0},{12,4},{16,24},{20,28},{24,16},{28,20},{1,9},{5... | collective-permute-start | bytes 786440 | tf_op jit(solution)/shard_map/ppermute | solution.py:23
  98.0 7.9 %collective-permute-start.2 = (bf16[64,2048]{1,0:T(8,128)(2,1)S(1)}, bf16[64,2048]{1,0:T(8,128)(2,1)S(1)}, u32[]{:S(2)}, u32[]{:S(2)}) collective-permute-start(bf16[64,2048]{1,0:T(8,128)(2,1)S(1)} %fusion.13), channel_id=1, source_target_pairs={{0,16},{4,20},{8,24},{12,28},{16,0},{20,4},{24,8},{28,12},{1,17},{... | collective-permute-start | bytes 786440 | tf_op jit(solution)/shard_map/ppermute | solution.py:23
  125.7 1.6 collective-permute-start.3
  127.3 8.4 %collective-permute-start.4 = (bf16[64,2048]{1,0:T(8,128)(2,1)S(1)}, bf16[64,2048]{1,0:T(8,128)(2,1)S(1)}, u32[]{:S(2)}, u32[]{:S(2)}) collective-permute-start(bf16[64,2048]{1,0:T(8,128)(2,1)S(1)} %fusion.15), channel_id=1, source_target_pairs={{0,8},{4,12},{8,0},{12,4},{16,24},{20,28},{24,16},{28,20},{1,9},{5... | collective-permute-start | bytes 786440 | tf_op jit(solution)/shard_map/ppermute | solution.py:23
  128.9 73.8 %all-gather.15.cloned.1.call-start = ((), (), s32[]{:S(2)}) async-start(), calls=%async_computation.3 | async-start | bytes 1310720 | tf_op jit(solution)/shard_map/all_gather | solution.py:14
  135.8 19.7 %copy-start.1 = (bf16[1,512,2048]{2,1,0:T(8,128)(2,1)S(1)}, bf16[1,512,2048]{2,1,0:T(8,128)(2,1)}, u32[]{:S(2)}) copy-start(bf16[1,512,2048]{2,1,0:T(8,128)(2,1)} %param.9) | copy-start | bytes 6291460
  135.9 7.6 %collective-permute-start.5 = (bf16[64,2048]{1,0:T(8,128)(2,1)S(1)}, bf16[64,2048]{1,0:T(8,128)(2,1)S(1)}, u32[]{:S(2)}, u32[]{:S(2)}) collective-permute-start(bf16[64,2048]{1,0:T(8,128)(2,1)S(1)} %fusion.16), channel_id=1, source_target_pairs={{0,16},{4,20},{8,24},{12,28},{16,0},{20,4},{24,8},{28,12},{1,17},{... | collective-permute-start | bytes 786440 | tf_op jit(solution)/shard_map/ppermute | solution.py:23
  155.5 14.0 %copy-start.3 = (bf16[2,64,2048]{2,1,0:T(8,128)(2,1)S(1)}, bf16[2,64,2048]{2,1,0:T(8,128)(2,1)}, u32[]{:S(2)}) copy-start(bf16[2,64,2048]{2,1,0:T(8,128)(2,1)} %param.11) | copy-start | bytes 1572868
  204.1 1.9 collective-permute-start.6
  206.1 8.8 %collective-permute-start.7 = (bf16[64,2048]{1,0:T(8,128)(2,1)S(1)}, bf16[64,2048]{1,0:T(8,128)(2,1)S(1)}, u32[]{:S(2)}, u32[]{:S(2)}) collective-permute-start(bf16[64,2048]{1,0:T(8,128)(2,1)S(1)} %fusion.12), channel_id=1, source_target_pairs={{0,8},{4,12},{8,0},{12,4},{16,24},{20,28},{24,16},{28,20},{1,9},{5... | collective-permute-start | bytes 786440 | tf_op jit(solution)/shard_map/ppermute | solution.py:23
  215.0 7.9 %collective-permute-start.8 = (bf16[64,2048]{1,0:T(8,128)(2,1)S(1)}, bf16[64,2048]{1,0:T(8,128)(2,1)S(1)}, u32[]{:S(2)}, u32[]{:S(2)}) collective-permute-start(bf16[64,2048]{1,0:T(8,128)(2,1)S(1)} %fusion.14), channel_id=1, source_target_pairs={{0,16},{4,20},{8,24},{12,28},{16,0},{20,4},{24,8},{28,12},{1,17},{... | collective-permute-start | bytes 786440 | tf_op jit(solution)/shard_map/ppermute | solution.py:23
  242.6 1.6 collective-permute-start.9
  244.3 8.4 %collective-permute-start.10 = (bf16[64,2048]{1,0:T(8,128)(2,1)S(1)}, bf16[64,2048]{1,0:T(8,128)(2,1)S(1)}, u32[]{:S(2)}, u32[]{:S(2)}) collective-permute-start(bf16[64,2048]{1,0:T(8,128)(2,1)S(1)} %fusion.17), channel_id=1, source_target_pairs={{0,8},{4,12},{8,0},{12,4},{16,24},{20,28},{24,16},{28,20},{1,9},{5... | collective-permute-start | bytes 786440 | tf_op jit(solution)/shard_map/ppermute | solution.py:23
  252.8 7.6 %collective-permute-start.11 = (bf16[64,2048]{1,0:T(8,128)(2,1)S(1)}, bf16[64,2048]{1,0:T(8,128)(2,1)S(1)}, u32[]{:S(2)}, u32[]{:S(2)}) collective-permute-start(bf16[64,2048]{1,0:T(8,128)(2,1)S(1)} %fusion.18), channel_id=1, source_target_pairs={{0,16},{4,20},{8,24},{12,28},{16,0},{20,4},{24,8},{28,12},{1,17},{... | collective-permute-start | bytes 786440 | tf_op jit(solution)/shard_map/ppermute | solution.py:23
Sparse Core Ops, SparseCore 0:
  8.9 30.6 all-gather.8
  57.7 27.3 all-gather.10
  129.0 26.4 all-gather.12
  175.3 27.3 all-gather.14
